TPU v7x, 256 devices: a whole 4x4x8 slice. The times are simulated.
256 devices in a mesh: grp: 8 (over y, core), row: 32 (over z, x).
Axes of the slice: x: 4, y: 4, z: 8, core: 2. Of those that a mesh axis runs over, the one named last changes fastest.
Arguments:
- fine_cols: int32 [10240, 5], P(('grp', 'row')), may hold values from 0 to 10239, as said below
- fine_blocks: bfloat16 [10240, 5, 128, 128], P(('grp', 'row'))
- prolong_cols: int32 [10240, 2], replicated, may hold values from 0 to 1023, as said below
- prolong_blocks: bfloat16 [10240, 2, 128, 128], P(('grp', 'row')), may hold values from -0.125 to 0.125
- agg_owner: int32 [1024], replicated, may hold values from 0 to 7, as said below
- coarse_rhs: float32 [1024, 128], P(('grp', 'row')), may hold values from -6 to 6
- lam_low: float32 [1], replicated, may hold values from 0.05 to 0.5
- lam_high: float32 [1], replicated, may hold values from 1.5 to 3.5
Outputs:
- coarse_operator: float32 [2048, 7, 128, 128], P(('grp', 'row'))
- coarse_solution: float32 [2048, 128], P(('grp', 'row'))
- coarse_residual: float32 [2048, 128], P(('grp', 'row'))
Inputs may be any that keep to these rules, and one draw needn't show every extreme that they name: fine_cols[i, 0] = i; the other 4 entries of row i are distinct rows (i + t) mod 10240 with 1 <= |t| <= 10; some row reaches |t| = 10. `prolong_cols`: the two entries of fine row i are two distinct ones of i // 10 - 1, i // 10, i // 10 + 1 in rising order, taken modulo 1024. `agg_owner`: the 4 aggregates made on one device go to distinct groups; for every row index some group owns one aggregate from each of the 8 groups at that row index.
All inputs are finite; a program needn't handle non-finite values.
Results may differ from a plain program's by a relative error of at most 0.0019.
Values may be sent and summed in bfloat16 or wider, within the bound.
A program may use at most 128 MiB of HBM per device.

v0:
```python
import jax
import jax.numpy as jnp
from jax import lax
from jax.sharding import PartitionSpec as P

HIGH = lax.Precision.HIGHEST


def extended_2(block, sides, width):
    for axis, dim in sides:
        count = lax.axis_size(axis)
        forward = [(i, i + 1) for i in range(count - 1)]
        forward.append((count - 1, 0))
        backward = [(target, source) for source, target in forward]
        low = lax.ppermute(
            lax.slice_in_dim(block, block.shape[dim] - width, None, axis=dim), axis, forward
        )
        high = lax.ppermute(lax.slice_in_dim(block, 0, width, axis=dim), axis, backward)
        block = jnp.concatenate([low, block, high], axis=dim)
    return block


def chebyshev_terms(lam_low, lam_high):
    center = 0.5 * (lam_high[0] + lam_low[0])
    radius = 0.5 * (lam_high[0] - lam_low[0])
    sigma_ratio = center / radius
    first_rho = 1.0 / sigma_ratio
    second_rho = 1.0 / (2.0 * sigma_ratio - first_rho)
    return (center, second_rho * first_rho, 2.0 * second_rho / radius)


def per_device(
    fine_cols, fine_blocks, prolong_cols, prolong_blocks, agg_owner, coarse_rhs, lam_low, lam_high
):
    rows_dev = fine_blocks.shape[0]
    band_width = fine_blocks.shape[2]
    groups = lax.axis_size("grp")
    rows_axis = lax.axis_size("row")
    devices = groups * rows_axis
    aggs_dev = coarse_rhs.shape[0]
    agg_rows = rows_dev // aggs_dev
    fine_total = rows_dev * devices
    coarse_total = aggs_dev * devices
    my_grp = lax.axis_index("grp")
    my_row = lax.axis_index("row")
    device = my_grp * rows_axis + my_row
    first_row = device * rows_dev
    offsets = jnp.arange(-2, 3, dtype=jnp.int32)
    group_ids = jnp.arange(groups, dtype=jnp.int32)
    p_pad = extended_2(prolong_blocks, ((("grp", "row"), 0),), agg_rows)
    pad_ids = (
        first_row - agg_rows + jnp.arange(rows_dev + 2 * agg_rows, dtype=jnp.int32)
    ) % fine_total
    cols_pad = jnp.take(prolong_cols, pad_ids, axis=0)

    def one_aggregate(agg_index):
        start = agg_index * agg_rows
        block_a = lax.dynamic_slice_in_dim(fine_blocks, start, agg_rows, 0)
        cols_here = lax.dynamic_slice_in_dim(fine_cols, start, agg_rows, 0)
        local_rows = start + jnp.arange(agg_rows, dtype=jnp.int32)
        global_rows = first_row + local_rows
        reach = (cols_here - global_rows[:, None] + agg_rows) % fine_total - agg_rows
        positions = local_rows[:, None] + agg_rows + reach
        p_near = jnp.take(p_pad, positions, axis=0)
        near_cols = jnp.take(cols_pad, positions, axis=0)
        agg_id = device * aggs_dev + agg_index
        shifted = (near_cols - agg_id + 2) % coarse_total - 2
        chosen = (shifted[..., None] == offsets).astype(jnp.float32)
        products = jnp.einsum(
            "iakm,iaqmn->iaqkn", block_a, p_near, preferred_element_type=jnp.float32
        )
        merged = jnp.einsum("iaqo,iaqkn->iokn", chosen, products, precision=HIGH).astype(
            jnp.bfloat16
        )
        own_blocks = lax.dynamic_slice_in_dim(prolong_blocks, start, agg_rows, 0)
        own_cols = lax.dynamic_slice_in_dim(cols_pad, start + agg_rows, agg_rows, 0)
        step_off = (own_cols - agg_id + 1) % coarse_total - 1
        term_blocks = jnp.einsum(
            "ipmk,iomn->ipokn", own_blocks, merged, preferred_element_type=jnp.float32
        )
        lifted = step_off[:, :, None, None, None]
        placing = (
            (lifted + 1 == jnp.arange(3, dtype=jnp.int32)[:, None])
            & (offsets[None, None, :, None, None] - lifted + 3 == jnp.arange(7, dtype=jnp.int32))
        ).astype(jnp.float32)
        return jnp.einsum("ipots,ipokn->tskn", placing, term_blocks, precision=HIGH)

    pieces = lax.map(one_aggregate, jnp.arange(aggs_dev, dtype=jnp.int32))
    partial_value = jnp.zeros((aggs_dev + 2, 7, band_width, band_width), jnp.float32)
    for target in range(3):
        partial_value = partial_value.at[target : target + aggs_dev].add(pieces[:, target])
    owners_mine = lax.dynamic_slice_in_dim(agg_owner, device * aggs_dev, aggs_dev, 0)
    send_onehot = (owners_mine[:, None] == group_ids).astype(jnp.float32)
    send_rhs = jnp.einsum("kg,kn->gn", send_onehot, coarse_rhs, precision=HIGH)
    extended = extended_2(partial_value, ((("grp", "row"), 0),), 1)
    native = partial_value[1 : aggs_dev + 1]
    native = native.at[0].add(extended[0])
    native = native.at[aggs_dev - 1].add(extended[aggs_dev + 3])
    send_rows = jnp.einsum("kg,ksmn->gsmn", send_onehot, native, precision=HIGH)
    got_rows, got_rhs = (
        lax.all_to_all(send_rows, "grp", split_axis=0, concat_axis=0, tiled=True),
        lax.all_to_all(send_rhs, "grp", split_axis=0, concat_axis=0, tiled=True),
    )
    source_dev = group_ids * rows_axis + my_row
    agg_table = source_dev[:, None] * aggs_dev + jnp.arange(aggs_dev, dtype=jnp.int32)
    matches = (jnp.take(agg_owner, agg_table, axis=0) == my_grp).astype(jnp.int32)
    slot_agg = source_dev * aggs_dev + jnp.sum(
        matches * jnp.arange(aggs_dev, dtype=jnp.int32), axis=1
    )
    near_ids = (slot_agg[:, None] + jnp.arange(7, dtype=jnp.int32) - 3) % coarse_total
    near_dev = near_ids // aggs_dev
    near_grp = near_dev // rows_axis
    near_row = near_dev % rows_axis
    near_owner = jnp.take(agg_owner, near_ids, axis=0)

    def operate(vector):
        whole = lax.all_gather(vector, ("grp", "row"), axis=0, tiled=True)
        nearby = jnp.take(whole, (near_owner * rows_axis + near_row) * groups + near_grp, axis=0)
        return jnp.einsum("gsmn,gsn->gm", got_rows, nearby, precision=HIGH)

    center, old_weight, resid_weight = chebyshev_terms(lam_low, lam_high)
    first_iter = got_rhs / center
    first_resid = got_rhs - operate(first_iter)
    second_iter = first_iter + old_weight * first_iter + resid_weight * first_resid
    second_resid = got_rhs - operate(second_iter)
    return (got_rows, second_iter, second_resid)


def solution(mesh):
    return jax.shard_map(
        per_device,
        mesh=mesh,
        in_specs=(
            P(("grp", "row"), None),
            P(("grp", "row"), None, None, None),
            P(),
            P(("grp", "row"), None, None, None),
            P(),
            P(("grp", "row"), None),
            P(),
            P(),
        ),
        out_specs=(
            P(("grp", "row"), None, None, None),
            P(("grp", "row"), None),
            P(("grp", "row"), None),
        ),
        check_vma=False,
    )
```

profile of v0, /device:TPU:1, one launch (start us, length us, event | category | flops | bytes accessed | tf_op | source)
XLA Modules:
  0.0 583.9 jit_solution(10987784176769533986)
XLA Ops:
  7.2 2.2 fusion.73
  9.4 2.0 collective-permute-start
  11.5 7.1 %collective-permute-start.1 = (bf16[10,2,128,128]{3,2,1,0:T(8,128)(2,1)S(1)}, bf16[10,2,128,128]{3,2,1,0:T(8,128)(2,1)}, u32[]{:S(2)}, u32[]{:S(2)}) collective-permute-start(bf16[10,2,128,128]{3,2,1,0:T(8,128)(2,1)S(1)} %get-tuple-element.460), channel_id=1, source_target_pairs={{1,0},{2,1},{3,2},{4,3},{5,4},{6,5},{7,6},{8,7},{9,8},{10,9},{11,1... | collective-permute-start | bytes 1966088 | tf_op jit(solution)/shard_map/ppermute | solution.py:18
  18.6 3.9 copy.53
  22.5 3.1 gather_fusion.2
  25.8 7.8 %collective-permute-done = bf16[10,2,128,128]{3,2,1,0:T(8,128)(2,1)} collective-permute-done((bf16[10,2,128,128]{3,2,1,0:T(8,128)(2,1)}, bf16[10,2,128,128]{3,2,1,0:T(8,128)(2,1)}, u32[]{:S(2)}, u32[]{:S(2)}) %collective-permute-start) | collective-permute-done | bytes 655392 | tf_op jit(solution)/shard_map/ppermute | solution.py:15
  33.6 3.3 pad_maximum_fusion
  36.9 265.3 %while.22 = (s32[]{:T(128)}, f32[4,3,7,128,128]{4,2,3,1,0:T(8,128)}, s32[4]{0:T(128)S(1)}, s32[60,2]{0,1:T(2,128)S(1)}, s32[]{:T(128)}, /*index=5*/s32[40,5]{0,1...) while((s32[]{:T(128)}, ...), condition=%wide.region_1.2_spmd.clone.clone, body=%wide.region_0.1_spmd.clone.clone.sunk | while | flops 1352506368 | bytes 91372768 | solution.py:88
  36.9 0.7 dynamic_slice.91
  38.7 4.9 gather_fusion
  43.6 4.3 copy.98
  47.8 5.2 fusion.101
  53.0 10.1 %copy.99 = f32[10,5,2,128,128]{4,1,2,3,0:T(8,128)} copy(f32[10,5,2,128,128]{3,4,2,1,0:T(8,128)} %fusion.101) | data formatting | bytes 13107200 | tf_op jit(solution)/shard_map/while/body/eval_jaxpr/iakm,iaqmn->iaqkn/transpose | solution.py:69
  64.8 10.6 %fusion.103 = bf16[10,5,128,128,1]{3,1,2,0,4:T(8,128)(2,1)S(1)} fusion(f32[10,5,2,128,128]{4,1,2,3,0:T(8,128)} %copy.99, s32[10,5,2]{1,2,0:T(2,128)S(1)} %copy.102, s32[5]{0:T(128)S(1)} %iota_add_fusion.3), kind=kOutput, calls=%fused_computation.16.clone.1 | convolution fusion | flops 99123696 | bytes 8192420 | tf_op jit(solution)/shard_map/while/body/eval_jaxpr/iaqo,iaqkn->iokn/dot_general | solution.py:72
  75.4 3.8 convolution_bitcast_fusion.2
  79.2 11.5 %copy.103 = f32[10,2,5,128,128]{4,0,1,2,3:T(8,128)} copy(f32[10,2,5,128,128]{3,4,1,2,0:T(8,128)} %convolution_bitcast_fusion.2) | data formatting | bytes 13107200 | tf_op jit(solution)/shard_map/while/body/eval_jaxpr/ipmk,iomn->ipokn/transpose | solution.py:78
  90.9 12.4 %bitcast_dynamic-update-slice_fusion.2 = f32[4,3,7,128,128]{4,2,3,1,0:T(8,128)} fusion(f32[4,3,7,128,128]{4,2,3,1,0:T(8,128)} %get-tuple-element.550, s32[]{:T(128)} %get-tuple-element.549, f32[10,2,5,128,128]{4,0,1,2,3:T(8,128)} %copy.103, pred[10,2,5,7]{0,3,1,2:T(8,128)(4,1)S(1)} %iota_compare_fusion.6, pred[10,2,3]{0,1,2:T(4,128)(4,1)S(1)} %iota_compare_fusion.7), kind=kOutput, calls=%fused_computation.21.clone.1 | convolution fusion | flops 412878912 | bytes 12059896 | tf_op jit(solution)/shard_map/while/body/eval_jaxpr/ipots,ipokn->tskn/dot_general | solution.py:86
  103.3 0.7 dynamic_slice.91
  105.0 4.9 gather_fusion
  109.9 4.3 copy.98
  114.2 5.2 fusion.101
  119.4 10.1 %copy.99 = f32[10,5,2,128,128]{4,1,2,3,0:T(8,128)} copy(f32[10,5,2,128,128]{3,4,2,1,0:T(8,128)} %fusion.101) | data formatting | bytes 13107200 | tf_op jit(solution)/shard_map/while/body/eval_jaxpr/iakm,iaqmn->iaqkn/transpose | solution.py:69
  131.1 10.6 %fusion.103 = bf16[10,5,128,128,1]{3,1,2,0,4:T(8,128)(2,1)S(1)} fusion(f32[10,5,2,128,128]{4,1,2,3,0:T(8,128)} %copy.99, s32[10,5,2]{1,2,0:T(2,128)S(1)} %copy.102, s32[5]{0:T(128)S(1)} %iota_add_fusion.3), kind=kOutput, calls=%fused_computation.16.clone.1 | convolution fusion | flops 99123696 | bytes 8192420 | tf_op jit(solution)/shard_map/while/body/eval_jaxpr/iaqo,iaqkn->iokn/dot_general | solution.py:72
  141.8 3.8 convolution_bitcast_fusion.2
  145.5 11.5 %copy.103 = f32[10,2,5,128,128]{4,0,1,2,3:T(8,128)} copy(f32[10,2,5,128,128]{3,4,1,2,0:T(8,128)} %convolution_bitcast_fusion.2) | data formatting | bytes 13107200 | tf_op jit(solution)/shard_map/while/body/eval_jaxpr/ipmk,iomn->ipokn/transpose | solution.py:78
  157.2 12.4 %bitcast_dynamic-update-slice_fusion.2 = f32[4,3,7,128,128]{4,2,3,1,0:T(8,128)} fusion(f32[4,3,7,128,128]{4,2,3,1,0:T(8,128)} %get-tuple-element.550, s32[]{:T(128)} %get-tuple-element.549, f32[10,2,5,128,128]{4,0,1,2,3:T(8,128)} %copy.103, pred[10,2,5,7]{0,3,1,2:T(8,128)(4,1)S(1)} %iota_compare_fusion.6, pred[10,2,3]{0,1,2:T(4,128)(4,1)S(1)} %iota_compare_fusion.7), kind=kOutput, calls=%fused_computation.21.clone.1 | convolution fusion | flops 412878912 | bytes 12059896 | tf_op jit(solution)/shard_map/while/body/eval_jaxpr/ipots,ipokn->tskn/dot_general | solution.py:86
  169.6 0.7 dynamic_slice.91
  171.3 4.9 gather_fusion
  176.2 4.3 copy.98
  180.5 5.2 fusion.101
  185.7 10.1 %copy.99 = f32[10,5,2,128,128]{4,1,2,3,0:T(8,128)} copy(f32[10,5,2,128,128]{3,4,2,1,0:T(8,128)} %fusion.101) | data formatting | bytes 13107200 | tf_op jit(solution)/shard_map/while/body/eval_jaxpr/iakm,iaqmn->iaqkn/transpose | solution.py:69
  197.4 10.6 %fusion.103 = bf16[10,5,128,128,1]{3,1,2,0,4:T(8,128)(2,1)S(1)} fusion(f32[10,5,2,128,128]{4,1,2,3,0:T(8,128)} %copy.99, s32[10,5,2]{1,2,0:T(2,128)S(1)} %copy.102, s32[5]{0:T(128)S(1)} %iota_add_fusion.3), kind=kOutput, calls=%fused_computation.16.clone.1 | convolution fusion | flops 99123696 | bytes 8192420 | tf_op jit(solution)/shard_map/while/body/eval_jaxpr/iaqo,iaqkn->iokn/dot_general | solution.py:72
  208.1 3.8 convolution_bitcast_fusion.2
  211.8 11.5 %copy.103 = f32[10,2,5,128,128]{4,0,1,2,3:T(8,128)} copy(f32[10,2,5,128,128]{3,4,1,2,0:T(8,128)} %convolution_bitcast_fusion.2) | data formatting | bytes 13107200 | tf_op jit(solution)/shard_map/while/body/eval_jaxpr/ipmk,iomn->ipokn/transpose | solution.py:78
  223.5 12.4 %bitcast_dynamic-update-slice_fusion.2 = f32[4,3,7,128,128]{4,2,3,1,0:T(8,128)} fusion(f32[4,3,7,128,128]{4,2,3,1,0:T(8,128)} %get-tuple-element.550, s32[]{:T(128)} %get-tuple-element.549, f32[10,2,5,128,128]{4,0,1,2,3:T(8,128)} %copy.103, pred[10,2,5,7]{0,3,1,2:T(8,128)(4,1)S(1)} %iota_compare_fusion.6, pred[10,2,3]{0,1,2:T(4,128)(4,1)S(1)} %iota_compare_fusion.7), kind=kOutput, calls=%fused_computation.21.clone.1 | convolution fusion | flops 412878912 | bytes 12059896 | tf_op jit(solution)/shard_map/while/body/eval_jaxpr/ipots,ipokn->tskn/dot_general | solution.py:86
  235.9 0.7 dynamic_slice.91
  237.6 4.9 gather_fusion
  242.5 4.3 copy.98
  246.7 5.2 fusion.101
  252.0 10.1 %copy.99 = f32[10,5,2,128,128]{4,1,2,3,0:T(8,128)} copy(f32[10,5,2,128,128]{3,4,2,1,0:T(8,128)} %fusion.101) | data formatting | bytes 13107200 | tf_op jit(solution)/shard_map/while/body/eval_jaxpr/iakm,iaqmn->iaqkn/transpose | solution.py:69
  263.7 10.6 %fusion.103 = bf16[10,5,128,128,1]{3,1,2,0,4:T(8,128)(2,1)S(1)} fusion(f32[10,5,2,128,128]{4,1,2,3,0:T(8,128)} %copy.99, s32[10,5,2]{1,2,0:T(2,128)S(1)} %copy.102, s32[5]{0:T(128)S(1)} %iota_add_fusion.3), kind=kOutput, calls=%fused_computation.16.clone.1 | convolution fusion | flops 99123696 | bytes 8192420 | tf_op jit(solution)/shard_map/while/body/eval_jaxpr/iaqo,iaqkn->iokn/dot_general | solution.py:72
  274.3 3.8 convolution_bitcast_fusion.2
  278.1 11.5 %copy.103 = f32[10,2,5,128,128]{4,0,1,2,3:T(8,128)} copy(f32[10,2,5,128,128]{3,4,1,2,0:T(8,128)} %convolution_bitcast_fusion.2) | data formatting | bytes 13107200 | tf_op jit(solution)/shard_map/while/body/eval_jaxpr/ipmk,iomn->ipokn/transpose | solution.py:78
  289.8 12.4 %bitcast_dynamic-update-slice_fusion.2 = f32[4,3,7,128,128]{4,2,3,1,0:T(8,128)} fusion(f32[4,3,7,128,128]{4,2,3,1,0:T(8,128)} %get-tuple-element.550, s32[]{:T(128)} %get-tuple-element.549, f32[10,2,5,128,128]{4,0,1,2,3:T(8,128)} %copy.103, pred[10,2,5,7]{0,3,1,2:T(8,128)(4,1)S(1)} %iota_compare_fusion.6, pred[10,2,3]{0,1,2:T(4,128)(4,1)S(1)} %iota_compare_fusion.7), kind=kOutput, calls=%fused_computation.21.clone.1 | convolution fusion | flops 412878912 | bytes 12059896 | tf_op jit(solution)/shard_map/while/body/eval_jaxpr/ipots,ipokn->tskn/dot_general | solution.py:86
  302.2 1.9 slice_bitcast_fusion.2
  304.3 1.3 copy-done.4
  306.8 17.2 %collective-permute-done.2 = f32[1,7,128,128]{3,1,2,0:T(8,128)S(1)} collective-permute-done((f32[1,7,128,128]{3,1,2,0:T(8,128)S(1)}, f32[1,7,128,128]{3,1,2,0:T(8,128)S(1)}, u32[]{:S(2)}, u32[]{:S(2)}) %collective-permute-start.2) | collective-permute-done | bytes 458784 | tf_op jit(solution)/shard_map/ppermute | solution.py:15
  324.3 0.9 fusion.65
  325.2 6.8 %all-to-all-start.1 = ((f32[8,1,128]{2,1,0:T(1,128)}), f32[8,1,128]{2,1,0:T(1,128)S(1)}, u32[]{:S(2)}, u32[]{:S(2)}) async-start(f32[8,1,128]{2,1,0:T(1,128)} %bitcast.7), calls=%async_computation.1 | async-start | bytes 8192 | tf_op jit(solution)/shard_map/all_to_all | solution.py:102
  332.0 2.4 collective-permute-done.3
  334.5 3.4 fusion.42
  337.9 2.5 copy.59
  340.4 9.1 %all-to-all-start = ((f32[8,7,128,128]{3,2,1,0:T(8,128)}), f32[8,7,128,128]{3,2,1,0:T(8,128)}, u32[]{:S(2)}, u32[]{:S(2)}) async-start(f32[8,7,128,128]{3,2,1,0:T(8,128)} %copy.59), calls=%async_computation | async-start | bytes 7340032 | tf_op jit(solution)/shard_map/all_to_all | solution.py:101
  352.0 0.7 gather_fusion.3
  353.1 0.7 gather_fusion.4
  354.2 101.2 %all-gather.3.cloned.1.call-done = f32[2048,128]{1,0:T(8,128)} async-done(((f32[8,128]{1,0:T(8,128)}), f32[2048,128]{1,0:T(8,128)}) %all-gather.3.cloned.1.call-update) | async-done | bytes 1048592 | tf_op jit(solution)/shard_map/all_gather | solution.py:117
  455.4 1.8 gather_fusion.5
  457.3 5.5 fusion.48
  462.9 0.6 fusion.50
  463.5 101.2 %all-gather.5.cloned.1.call-done = f32[2048,128]{1,0:T(8,128)} async-done(((f32[8,128]{1,0:T(8,128)}), f32[2048,128]{1,0:T(8,128)}) %all-gather.5.cloned.1.call-update) | async-done | bytes 1048592 | tf_op jit(solution)/shard_map/all_gather | solution.py:117
  564.7 1.8 gather_fusion.6
  566.6 5.6 fusion.46
  572.1 0.6 sub.134
  572.8 4.3 copy.118
  (129 shorter events, 9.6 us)
Async XLA Ops:
  7.2 317.2 %copy-start = (f32[4,128]{1,0:T(4,128)S(1)}, f32[4,128]{1,0:T(4,128)}, u32[]{:S(2)}) copy-start(f32[4,128]{1,0:T(4,128)} %param.27) | copy-start | bytes 6148
  9.4 24.2 %copy-start.2 = (bf16[40,2,128,128]{3,2,1,0:T(8,128)(2,1)S(1)}, bf16[40,2,128,128]{3,2,1,0:T(8,128)(2,1)}, u32[]{:S(2)}) copy-start(bf16[40,2,128,128]{3,2,1,0:T(8,128)(2,1)} %param.25) | copy-start | bytes 7864324
  9.4 24.2 %collective-permute-start = (bf16[10,2,128,128]{3,2,1,0:T(8,128)(2,1)}, bf16[10,2,128,128]{3,2,1,0:T(8,128)(2,1)}, u32[]{:S(2)}, u32[]{:S(2)}) collective-permute-start(bf16[10,2,128,128]{3,2,1,0:T(8,128)(2,1)} %get-tuple-element.459), channel_id=1, source_target_pairs={{0,1},{1,2},{2,3},{3,4},{4,5},{5,6},{6,7},{7,8},{8,9},{9,10},{10,1... | collective-permute-start | bytes 1966088 | tf_op jit(solution)/shard_map/ppermute | solution.py:15
  11.5 22.2 %collective-permute-start.1 = (bf16[10,2,128,128]{3,2,1,0:T(8,128)(2,1)S(1)}, bf16[10,2,128,128]{3,2,1,0:T(8,128)(2,1)}, u32[]{:S(2)}, u32[]{:S(2)}) collective-permute-start(bf16[10,2,128,128]{3,2,1,0:T(8,128)(2,1)S(1)} %get-tuple-element.460), channel_id=1, source_target_pairs={{1,0},{2,1},{3,2},{4,3},{5,4},{6,5},{7,6},{8,7},{9,8},{10,9},{11,1... | collective-permute-start | bytes 1966088 | tf_op jit(solution)/shard_map/ppermute | solution.py:18
  25.8 11.1 %copy-start.5 = (s32[40,5]{0,1:T(8,128)S(1)}, s32[40,5]{0,1:T(8,128)}, u32[]{:S(2)}) copy-start(s32[40,5]{0,1:T(8,128)} %param.22) | copy-start | bytes 2404
  64.8 10.6 %copy-start.3 = (bf16[40,2,128,128]{3,2,1,0:T(8,128)(2,1)S(1)}, bf16[40,2,128,128]{3,2,1,0:T(8,128)(2,1)}, u32[]{:S(2)}) copy-start(bf16[40,2,128,128]{3,2,1,0:T(8,128)(2,1)} %get-tuple-element.602) | copy-start | bytes 7864324 | tf_op jit(solution)/shard_map/while
  131.1 10.6 %copy-start.3 = (bf16[40,2,128,128]{3,2,1,0:T(8,128)(2,1)S(1)}, bf16[40,2,128,128]{3,2,1,0:T(8,128)(2,1)}, u32[]{:S(2)}) copy-start(bf16[40,2,128,128]{3,2,1,0:T(8,128)(2,1)} %get-tuple-element.602) | copy-start | bytes 7864324 | tf_op jit(solution)/shard_map/while
  197.4 10.6 %copy-start.3 = (bf16[40,2,128,128]{3,2,1,0:T(8,128)(2,1)S(1)}, bf16[40,2,128,128]{3,2,1,0:T(8,128)(2,1)}, u32[]{:S(2)}) copy-start(bf16[40,2,128,128]{3,2,1,0:T(8,128)(2,1)} %get-tuple-element.602) | copy-start | bytes 7864324 | tf_op jit(solution)/shard_map/while
  263.7 10.6 %copy-start.3 = (bf16[40,2,128,128]{3,2,1,0:T(8,128)(2,1)S(1)}, bf16[40,2,128,128]{3,2,1,0:T(8,128)(2,1)}, u32[]{:S(2)}) copy-start(bf16[40,2,128,128]{3,2,1,0:T(8,128)(2,1)} %get-tuple-element.602) | copy-start | bytes 7864324 | tf_op jit(solution)/shard_map/while
  302.2 3.4 copy-start.4
  306.4 17.6 %collective-permute-start.2 = (f32[1,7,128,128]{3,1,2,0:T(8,128)S(1)}, f32[1,7,128,128]{3,1,2,0:T(8,128)S(1)}, u32[]{:S(2)}, u32[]{:S(2)}) collective-permute-start(f32[1,7,128,128]{3,1,2,0:T(8,128)S(1)} %slice.195), channel_id=1, source_target_pairs={{0,1},{1,2},{2,3},{3,4},{4,5},{5,6},{6,7},{7,8},{8,9},{9,10},{10,1... | collective-permute-start | bytes 1376264 | tf_op jit(solution)/shard_map/ppermute | solution.py:15
  306.6 17.7 %copy-start.1 = (s32[1024]{0:T(1024)S(1)}, s32[1024]{0:T(1024)}, u32[]{:S(2)}) copy-start(s32[1024]{0:T(1024)} %param.26) | copy-start | bytes 12292
  324.2 10.2 %collective-permute-start.3 = (f32[1,7,128,128]{3,1,2,0:T(8,128)S(1)}, f32[1,7,128,128]{3,1,2,0:T(8,128)S(1)}, u32[]{:S(2)}, u32[]{:S(2)}) collective-permute-start(f32[1,7,128,128]{3,1,2,0:T(8,128)S(1)} %get-tuple-element.457), channel_id=1, source_target_pairs={{1,0},{2,1},{3,2},{4,3},{5,4},{6,5},{7,6},{8,7},{9,8},{10,9},{11,1... | collective-permute-start | bytes 1376264 | tf_op jit(solution)/shard_map/ppermute | solution.py:18
  325.2 15.2 %all-to-all-start.1 = ((f32[8,1,128]{2,1,0:T(1,128)}), f32[8,1,128]{2,1,0:T(1,128)S(1)}, u32[]{:S(2)}, u32[]{:S(2)}) async-start(f32[8,1,128]{2,1,0:T(1,128)} %bitcast.7), calls=%async_computation.1 | async-start | bytes 8192 | tf_op jit(solution)/shard_map/all_to_all | solution.py:102
  340.4 117.0 %all-to-all-start = ((f32[8,7,128,128]{3,2,1,0:T(8,128)}), f32[8,7,128,128]{3,2,1,0:T(8,128)}, u32[]{:S(2)}, u32[]{:S(2)}) async-start(f32[8,7,128,128]{3,2,1,0:T(8,128)} %copy.59), calls=%async_computation | async-start | bytes 7340032 | tf_op jit(solution)/shard_map/all_to_all | solution.py:101
  349.5 106.0 %all-gather.3.cloned.1.call-start = ((), (), s32[]{:S(2)}) async-start(), calls=%async_computation.2 | async-start | bytes 1052672 | tf_op jit(solution)/shard_map/all_gather | solution.py:117
  351.4 213.3 %all-gather.5.cloned.1.call-start = ((), (), s32[]{:S(2)}) async-start(), calls=%async_computation.3 | async-start | bytes 1052672 | tf_op jit(solution)/shard_map/all_gather | solution.py:117
Sparse Core Ops, SparseCore 0:
  354.6 100.8 all-gather.2
  463.7 100.9 all-gather.4
where the time goes:
time: 587 us; the launch traced here: 584 us
  waiting for transfers between devices  230 us (39%)
  local copies, waits for them, and re-layouts  156 us (27%)
  matrix products  143 us (24%)
  starting transfers between devices  25.5 us (4%)
  between operations  15.7 us (3%)
  other arithmetic  8.03 us (1%)
  loops' own time  5.94 us (1%)
    all_gather x2, waiting for transfers between devices, operate(): whole = lax.all_gather(vector, ('grp', 'row'), axis=0, tiled=True)  202 us
    dot_general x4, matrix products, one_aggregate(): return jnp.einsum('ipots,ipokn->tskn', placing, term_blocks, precision=HIGH)  49.6 us
    transpose x4, local copies, waits for them, and re-layouts, one_aggregate(): jnp.einsum('ipmk,iomn->ipokn', own_blocks, merged, preferred_element_type...  45.9 us
    dot_general x4, matrix products, one_aggregate(): jnp.einsum('iaqo,iaqkn->iokn', chosen, products, precision=HIGH)  42.5 us
    transpose x4, local copies, waits for them, and re-layouts, one_aggregate(): jnp.einsum('iakm,iaqmn->iaqkn', block_a, p_near, preferred_element_type=j...  40.5 us
    gather x8, local copies, waits for them, and re-layouts, one_aggregate(): p_near = jnp.take(p_pad, positions, axis=0)  36.6 us
    ppermute x2, waiting for transfers between devices, extended_2(): lax.ppermute(lax.slice_in_dim(block, block.shape[dim] - width, None, axis...  25.1 us
    dot_general x4, matrix products, one_aggregate(): jnp.einsum('iakm,iaqmn->iaqkn', block_a, p_near, preferred_element_type=j...  20.8 us
  transfers between devices with their start and end apart: 8, of which 5 were waited for; matrix products, arithmetic and copies ran while one was open for 3% of the time, Pallas kernels for 0%

commit v1 on v0

--- a/solution.py
+++ b/solution.py
@@ -114,7 +114,12 @@
     near_owner = jnp.take(agg_owner, near_ids, axis=0)
 
     def operate(vector):
-        whole = lax.all_gather(vector, ("grp", "row"), axis=0, tiled=True)
+        whole = jnp.concatenate(
+            lax.all_to_all(
+                jnp.stack([vector] * lax.axis_size(("grp", "row"))), ("grp", "row"), 0, 0
+            ),
+            axis=0,
+        )
         nearby = jnp.take(whole, (near_owner * rows_axis + near_row) * groups + near_grp, axis=0)
         return jnp.einsum("gsmn,gsn->gm", got_rows, nearby, precision=HIGH)
 

time: 587 us -> 458 us (0.78)
  waiting for transfers between devices: 230 us -> 66.1 us
  blocking collectives: 0 us -> 39.3 us
  between operations: 15.7 us -> 2.36 us
  starting transfers between devices: 25.5 us -> 34.8 us
    all_gather x2 -> x0, waiting for transfers between devices: 202 us -> none  [operate(): whole = lax.all_gather(vector, ('grp', 'row'), axis=0, tiled=True)]
    all_to_all x0 -> x1, blocking collectives: none -> 39.3 us  [operate(): lax.all_to_all(jnp.stack([vector] * lax.axis_size(('grp', 'row'))), ('grp...]
    all_to_all x1, waiting for transfers between devices: 0.01 us -> 38.9 us  [per_device(): lax.all_to_all(send_rows, 'grp', split_axis=0, concat_axis=0, tiled=True)]
    all_to_all x0 -> x1, starting transfers between devices: none -> 9.69 us  [operate(): lax.all_to_all(jnp.stack([vector] * lax.axis_size(('grp', 'row'))), ('grp...]
    ppermute x2, waiting for transfers between devices: 25.1 us -> 17.3 us  [extended_2(): lax.ppermute(lax.slice_in_dim(block, block.shape[dim] - width, None, axis...]
    ppermute x2, waiting for transfers between devices: 2.4 us -> 9.9 us  [extended_2(): lax.ppermute(lax.slice_in_dim(block, 0, width, axis=dim), axis, backward)]
  transfers between devices with their start and end apart: 8 -> 7, of which waited for: 5 -> 3; matrix products, arithmetic and copies ran while one was open for 3% -> 63% of each run, Pallas kernels for 0% -> 0%
where the time goes in v1:
time: 458 us; the launch traced here: 455 us
  local copies, waits for them, and re-layouts  156 us (34%)
  matrix products  143 us (31%)
  waiting for transfers between devices  66.1 us (14%)
  blocking collectives  39.3 us (9%)
  starting transfers between devices  34.8 us (8%)
  other arithmetic  6.83 us (1%)
  loops' own time  6.1 us (1%)
    dot_general x4, matrix products, one_aggregate(): return jnp.einsum('ipots,ipokn->tskn', placing, term_blocks, precision=HIGH)  49.6 us
    transpose x4, local copies, waits for them, and re-layouts, one_aggregate(): jnp.einsum('ipmk,iomn->ipokn', own_blocks, merged, preferred_element_type...  45.9 us
    dot_general x4, matrix products, one_aggregate(): jnp.einsum('iaqo,iaqkn->iokn', chosen, products, precision=HIGH)  42.5 us
    transpose x4, local copies, waits for them, and re-layouts, one_aggregate(): jnp.einsum('iakm,iaqmn->iaqkn', block_a, p_near, preferred_element_type=j...  40.5 us
    all_to_all x1, blocking collectives, operate(): lax.all_to_all(jnp.stack([vector] * lax.axis_size(('grp', 'row'))), ('grp...  39.3 us
    all_to_all x1, waiting for transfers between devices, per_device(): lax.all_to_all(send_rows, 'grp', split_axis=0, concat_axis=0, tiled=True)  38.9 us
    gather x8, local copies, waits for them, and re-layouts, one_aggregate(): p_near = jnp.take(p_pad, positions, axis=0)  36.6 us
    dot_general x4, matrix products, one_aggregate(): jnp.einsum('iakm,iaqmn->iaqkn', block_a, p_near, preferred_element_type=j...  20.8 us
  transfers between devices with their start and end apart: 7, of which 3 were waited for; matrix products, arithmetic and copies ran while one was open for 63% of the time, Pallas kernels for 0%

profile of v1, /device:TPU:1, one launch (start us, length us, event | category | flops | bytes accessed | tf_op | source)
XLA Modules:
  0.0 455.1 jit_solution(12432597916977112288)
XLA Ops:
  0.6 2.2 fusion.73
  2.9 2.0 collective-permute-start
  4.9 7.1 %collective-permute-start.1 = (bf16[10,2,128,128]{3,2,1,0:T(8,128)(2,1)S(1)}, bf16[10,2,128,128]{3,2,1,0:T(8,128)(2,1)}, u32[]{:S(2)}, u32[]{:S(2)}) collective-permute-start(bf16[10,2,128,128]{3,2,1,0:T(8,128)(2,1)S(1)} %get-tuple-element.460), channel_id=1, source_target_pairs={{1,0},{2,1},{3,2},{4,3},{5,4},{6,5},{7,6},{8,7},{9,8},{10,9},{11,1... | collective-permute-start | bytes 1966088 | tf_op jit(solution)/shard_map/ppermute | solution.py:18
  12.1 0.8 dynamic_slice.54
  12.8 0.8 fusion.65
  13.7 5.5 %all-to-all-start.1 = ((f32[8,1,128]{2,1,0:T(1,128)}), f32[8,1,128]{2,1,0:T(1,128)S(1)}, u32[]{:S(2)}, u32[]{:S(2)}) async-start(f32[8,1,128]{2,1,0:T(1,128)} %bitcast.7), calls=%async_computation.1 | async-start | bytes 8192 | tf_op jit(solution)/shard_map/all_to_all | solution.py:102
  19.2 4.1 copy.53
  23.3 3.1 gather_fusion.2
  27.9 1.1 stack.4
  28.9 9.7 %all-to-all-start.2 = ((f32[256,8,128]{2,1,0:T(8,128)}), f32[256,8,128]{2,1,0:T(8,128)}, u32[]{:S(2)}, u32[]{:S(2)}) async-start(f32[256,8,128]{2,1,0:T(8,128)} %stack.4), calls=%async_computation.2 | async-start | bytes 2097152 | tf_op jit(solution)/shard_map/all_to_all | solution.py:118
  38.7 3.3 pad_maximum_fusion
  42.0 265.4 %while.22 = (s32[]{:T(128)}, f32[4,3,7,128,128]{4,2,3,1,0:T(8,128)}, s32[4]{0:T(128)S(1)}, s32[60,2]{0,1:T(2,128)S(1)}, s32[]{:T(128)}, /*index=5*/s32[40,5]{0,1...) while((s32[]{:T(128)}, ...), condition=%wide.region_1.2_spmd.clone.clone, body=%wide.region_0.1_spmd.clone.clone.sunk | while | flops 1352506368 | bytes 91372768 | solution.py:88
  42.2 0.7 dynamic_slice.91
  43.9 4.9 %gather_fusion = bf16[50,2,128,128]{3,2,1,0:T(8,128)(2,1)} fusion(bf16[60,2,128,128]{3,2,1,0:T(8,128)(2,1)} %get-tuple-element.571, s32[1024]{0:T(1024)S(1)} %pad_clamp_fusion.6), kind=kCustom, calls=%fused_computation.2.clone.clone.1 | custom fusion | bytes 6553800 | tf_op jit(solution)/shard_map/while/body/eval_jaxpr/jit(_take)/gather | solution.py:64
  48.8 4.3 copy.98
  53.1 5.2 %fusion.101 = f32[10,5,2,128,128]{3,4,2,1,0:T(8,128)} fusion(bf16[10,5,2,128,128]{3,4,2,1,0:T(8,128)(2,1)S(1)} %copy.98, pred[10,5]{1,0:T(8,128)(4,1)S(1)} %get-tuple-element.531, bf16[40,5,128,128]{3,2,1,0:T(8,128)(2,1)} %get-tuple-element.572, s32[]{:T(128)S(6)} %select_n.363), kind=kOutput, calls=%fused_computation.14.clone.1 | convolution fusion | flops 421068800 | bytes 11468854 | tf_op jit(solution)/shard_map/while/body/eval_jaxpr/iakm,iaqmn->iaqkn/dot_general | solution.py:69
  58.3 10.1 %copy.99 = f32[10,5,2,128,128]{4,1,2,3,0:T(8,128)} copy(f32[10,5,2,128,128]{3,4,2,1,0:T(8,128)} %fusion.101) | data formatting | bytes 13107200 | tf_op jit(solution)/shard_map/while/body/eval_jaxpr/iakm,iaqmn->iaqkn/transpose | solution.py:69
  70.0 10.6 %fusion.103 = bf16[10,5,128,128,1]{3,1,2,0,4:T(8,128)(2,1)S(1)} fusion(f32[10,5,2,128,128]{4,1,2,3,0:T(8,128)} %copy.99, s32[10,5,2]{1,2,0:T(2,128)S(1)} %copy.102, s32[5]{0:T(128)S(1)} %iota_add_fusion.3), kind=kOutput, calls=%fused_computation.16.clone.1 | convolution fusion | flops 99123696 | bytes 8192420 | tf_op jit(solution)/shard_map/while/body/eval_jaxpr/iaqo,iaqkn->iokn/dot_general | solution.py:72
  80.6 3.8 convolution_bitcast_fusion.2
  84.4 11.5 %copy.103 = f32[10,2,5,128,128]{4,0,1,2,3:T(8,128)} copy(f32[10,2,5,128,128]{3,4,1,2,0:T(8,128)} %convolution_bitcast_fusion.2) | data formatting | bytes 13107200 | tf_op jit(solution)/shard_map/while/body/eval_jaxpr/ipmk,iomn->ipokn/transpose | solution.py:78
  96.1 12.4 %bitcast_dynamic-update-slice_fusion.2 = f32[4,3,7,128,128]{4,2,3,1,0:T(8,128)} fusion(f32[4,3,7,128,128]{4,2,3,1,0:T(8,128)} %get-tuple-element.550, s32[]{:T(128)} %get-tuple-element.549, f32[10,2,5,128,128]{4,0,1,2,3:T(8,128)} %copy.103, pred[10,2,5,7]{0,3,1,2:T(8,128)(4,1)S(1)} %iota_compare_fusion.6, pred[10,2,3]{0,1,2:T(4,128)(4,1)S(1)} %iota_compare_fusion.7), kind=kOutput, calls=%fused_computation.21.clone.1 | convolution fusion | flops 412878912 | bytes 12059896 | tf_op jit(solution)/shard_map/while/body/eval_jaxpr/ipots,ipokn->tskn/dot_general | solution.py:86
  108.5 0.7 dynamic_slice.91
  110.2 4.9 %gather_fusion = bf16[50,2,128,128]{3,2,1,0:T(8,128)(2,1)} fusion(bf16[60,2,128,128]{3,2,1,0:T(8,128)(2,1)} %get-tuple-element.571, s32[1024]{0:T(1024)S(1)} %pad_clamp_fusion.6), kind=kCustom, calls=%fused_computation.2.clone.clone.1 | custom fusion | bytes 6553800 | tf_op jit(solution)/shard_map/while/body/eval_jaxpr/jit(_take)/gather | solution.py:64
  115.1 4.3 copy.98
  119.4 5.2 %fusion.101 = f32[10,5,2,128,128]{3,4,2,1,0:T(8,128)} fusion(bf16[10,5,2,128,128]{3,4,2,1,0:T(8,128)(2,1)S(1)} %copy.98, pred[10,5]{1,0:T(8,128)(4,1)S(1)} %get-tuple-element.531, bf16[40,5,128,128]{3,2,1,0:T(8,128)(2,1)} %get-tuple-element.572, s32[]{:T(128)S(6)} %select_n.363), kind=kOutput, calls=%fused_computation.14.clone.1 | convolution fusion | flops 421068800 | bytes 11468854 | tf_op jit(solution)/shard_map/while/body/eval_jaxpr/iakm,iaqmn->iaqkn/dot_general | solution.py:69
  124.6 10.1 %copy.99 = f32[10,5,2,128,128]{4,1,2,3,0:T(8,128)} copy(f32[10,5,2,128,128]{3,4,2,1,0:T(8,128)} %fusion.101) | data formatting | bytes 13107200 | tf_op jit(solution)/shard_map/while/body/eval_jaxpr/iakm,iaqmn->iaqkn/transpose | solution.py:69
  136.3 10.6 %fusion.103 = bf16[10,5,128,128,1]{3,1,2,0,4:T(8,128)(2,1)S(1)} fusion(f32[10,5,2,128,128]{4,1,2,3,0:T(8,128)} %copy.99, s32[10,5,2]{1,2,0:T(2,128)S(1)} %copy.102, s32[5]{0:T(128)S(1)} %iota_add_fusion.3), kind=kOutput, calls=%fused_computation.16.clone.1 | convolution fusion | flops 99123696 | bytes 8192420 | tf_op jit(solution)/shard_map/while/body/eval_jaxpr/iaqo,iaqkn->iokn/dot_general | solution.py:72
  147.0 3.8 convolution_bitcast_fusion.2
  150.7 11.5 %copy.103 = f32[10,2,5,128,128]{4,0,1,2,3:T(8,128)} copy(f32[10,2,5,128,128]{3,4,1,2,0:T(8,128)} %convolution_bitcast_fusion.2) | data formatting | bytes 13107200 | tf_op jit(solution)/shard_map/while/body/eval_jaxpr/ipmk,iomn->ipokn/transpose | solution.py:78
  162.4 12.4 %bitcast_dynamic-update-slice_fusion.2 = f32[4,3,7,128,128]{4,2,3,1,0:T(8,128)} fusion(f32[4,3,7,128,128]{4,2,3,1,0:T(8,128)} %get-tuple-element.550, s32[]{:T(128)} %get-tuple-element.549, f32[10,2,5,128,128]{4,0,1,2,3:T(8,128)} %copy.103, pred[10,2,5,7]{0,3,1,2:T(8,128)(4,1)S(1)} %iota_compare_fusion.6, pred[10,2,3]{0,1,2:T(4,128)(4,1)S(1)} %iota_compare_fusion.7), kind=kOutput, calls=%fused_computation.21.clone.1 | convolution fusion | flops 412878912 | bytes 12059896 | tf_op jit(solution)/shard_map/while/body/eval_jaxpr/ipots,ipokn->tskn/dot_general | solution.py:86
  176.5 4.9 %gather_fusion = bf16[50,2,128,128]{3,2,1,0:T(8,128)(2,1)} fusion(bf16[60,2,128,128]{3,2,1,0:T(8,128)(2,1)} %get-tuple-element.571, s32[1024]{0:T(1024)S(1)} %pad_clamp_fusion.6), kind=kCustom, calls=%fused_computation.2.clone.clone.1 | custom fusion | bytes 6553800 | tf_op jit(solution)/shard_map/while/body/eval_jaxpr/jit(_take)/gather | solution.py:64
  181.4 4.3 copy.98
  185.7 5.2 %fusion.101 = f32[10,5,2,128,128]{3,4,2,1,0:T(8,128)} fusion(bf16[10,5,2,128,128]{3,4,2,1,0:T(8,128)(2,1)S(1)} %copy.98, pred[10,5]{1,0:T(8,128)(4,1)S(1)} %get-tuple-element.531, bf16[40,5,128,128]{3,2,1,0:T(8,128)(2,1)} %get-tuple-element.572, s32[]{:T(128)S(6)} %select_n.363), kind=kOutput, calls=%fused_computation.14.clone.1 | convolution fusion | flops 421068800 | bytes 11468854 | tf_op jit(solution)/shard_map/while/body/eval_jaxpr/iakm,iaqmn->iaqkn/dot_general | solution.py:69
  190.9 10.1 %copy.99 = f32[10,5,2,128,128]{4,1,2,3,0:T(8,128)} copy(f32[10,5,2,128,128]{3,4,2,1,0:T(8,128)} %fusion.101) | data formatting | bytes 13107200 | tf_op jit(solution)/shard_map/while/body/eval_jaxpr/iakm,iaqmn->iaqkn/transpose | solution.py:69
  202.6 10.6 %fusion.103 = bf16[10,5,128,128,1]{3,1,2,0,4:T(8,128)(2,1)S(1)} fusion(f32[10,5,2,128,128]{4,1,2,3,0:T(8,128)} %copy.99, s32[10,5,2]{1,2,0:T(2,128)S(1)} %copy.102, s32[5]{0:T(128)S(1)} %iota_add_fusion.3), kind=kOutput, calls=%fused_computation.16.clone.1 | convolution fusion | flops 99123696 | bytes 8192420 | tf_op jit(solution)/shard_map/while/body/eval_jaxpr/iaqo,iaqkn->iokn/dot_general | solution.py:72
  213.3 3.8 convolution_bitcast_fusion.2
  217.0 11.5 %copy.103 = f32[10,2,5,128,128]{4,0,1,2,3:T(8,128)} copy(f32[10,2,5,128,128]{3,4,1,2,0:T(8,128)} %convolution_bitcast_fusion.2) | data formatting | bytes 13107200 | tf_op jit(solution)/shard_map/while/body/eval_jaxpr/ipmk,iomn->ipokn/transpose | solution.py:78
  228.7 12.4 %bitcast_dynamic-update-slice_fusion.2 = f32[4,3,7,128,128]{4,2,3,1,0:T(8,128)} fusion(f32[4,3,7,128,128]{4,2,3,1,0:T(8,128)} %get-tuple-element.550, s32[]{:T(128)} %get-tuple-element.549, f32[10,2,5,128,128]{4,0,1,2,3:T(8,128)} %copy.103, pred[10,2,5,7]{0,3,1,2:T(8,128)(4,1)S(1)} %iota_compare_fusion.6, pred[10,2,3]{0,1,2:T(4,128)(4,1)S(1)} %iota_compare_fusion.7), kind=kOutput, calls=%fused_computation.21.clone.1 | convolution fusion | flops 412878912 | bytes 12059896 | tf_op jit(solution)/shard_map/while/body/eval_jaxpr/ipots,ipokn->tskn/dot_general | solution.py:86
  241.1 0.7 dynamic_slice.91
  242.8 4.9 %gather_fusion = bf16[50,2,128,128]{3,2,1,0:T(8,128)(2,1)} fusion(bf16[60,2,128,128]{3,2,1,0:T(8,128)(2,1)} %get-tuple-element.571, s32[1024]{0:T(1024)S(1)} %pad_clamp_fusion.6), kind=kCustom, calls=%fused_computation.2.clone.clone.1 | custom fusion | bytes 6553800 | tf_op jit(solution)/shard_map/while/body/eval_jaxpr/jit(_take)/gather | solution.py:64
  247.7 4.3 copy.98
  252.0 5.2 %fusion.101 = f32[10,5,2,128,128]{3,4,2,1,0:T(8,128)} fusion(bf16[10,5,2,128,128]{3,4,2,1,0:T(8,128)(2,1)S(1)} %copy.98, pred[10,5]{1,0:T(8,128)(4,1)S(1)} %get-tuple-element.531, bf16[40,5,128,128]{3,2,1,0:T(8,128)(2,1)} %get-tuple-element.572, s32[]{:T(128)S(6)} %select_n.363), kind=kOutput, calls=%fused_computation.14.clone.1 | convolution fusion | flops 421068800 | bytes 11468854 | tf_op jit(solution)/shard_map/while/body/eval_jaxpr/iakm,iaqmn->iaqkn/dot_general | solution.py:69
  257.2 10.1 %copy.99 = f32[10,5,2,128,128]{4,1,2,3,0:T(8,128)} copy(f32[10,5,2,128,128]{3,4,2,1,0:T(8,128)} %fusion.101) | data formatting | bytes 13107200 | tf_op jit(solution)/shard_map/while/body/eval_jaxpr/iakm,iaqmn->iaqkn/transpose | solution.py:69
  268.9 10.6 %fusion.103 = bf16[10,5,128,128,1]{3,1,2,0,4:T(8,128)(2,1)S(1)} fusion(f32[10,5,2,128,128]{4,1,2,3,0:T(8,128)} %copy.99, s32[10,5,2]{1,2,0:T(2,128)S(1)} %copy.102, s32[5]{0:T(128)S(1)} %iota_add_fusion.3), kind=kOutput, calls=%fused_computation.16.clone.1 | convolution fusion | flops 99123696 | bytes 8192420 | tf_op jit(solution)/shard_map/while/body/eval_jaxpr/iaqo,iaqkn->iokn/dot_general | solution.py:72
  279.5 3.8 convolution_bitcast_fusion.2
  283.3 11.5 %copy.103 = f32[10,2,5,128,128]{4,0,1,2,3:T(8,128)} copy(f32[10,2,5,128,128]{3,4,1,2,0:T(8,128)} %convolution_bitcast_fusion.2) | data formatting | bytes 13107200 | tf_op jit(solution)/shard_map/while/body/eval_jaxpr/ipmk,iomn->ipokn/transpose | solution.py:78
  295.0 12.4 %bitcast_dynamic-update-slice_fusion.2 = f32[4,3,7,128,128]{4,2,3,1,0:T(8,128)} fusion(f32[4,3,7,128,128]{4,2,3,1,0:T(8,128)} %get-tuple-element.550, s32[]{:T(128)} %get-tuple-element.549, f32[10,2,5,128,128]{4,0,1,2,3:T(8,128)} %copy.103, pred[10,2,5,7]{0,3,1,2:T(8,128)(4,1)S(1)} %iota_compare_fusion.6, pred[10,2,3]{0,1,2:T(4,128)(4,1)S(1)} %iota_compare_fusion.7), kind=kOutput, calls=%fused_computation.21.clone.1 | convolution fusion | flops 412878912 | bytes 12059896 | tf_op jit(solution)/shard_map/while/body/eval_jaxpr/ipots,ipokn->tskn/dot_general | solution.py:86
  307.4 1.9 slice_bitcast_fusion.2
  309.5 1.3 copy-done.5
  311.6 1.5 collective-permute-start.2
  313.3 17.3 %collective-permute-done.2 = f32[1,7,128,128]{3,1,2,0:T(8,128)S(1)} collective-permute-done((f32[1,7,128,128]{3,1,2,0:T(8,128)S(1)}, f32[1,7,128,128]{3,1,2,0:T(8,128)S(1)}, u32[]{:S(2)}, u32[]{:S(2)}) %collective-permute-start.2) | collective-permute-done | bytes 458784 | tf_op jit(solution)/shard_map/ppermute | solution.py:15
  330.8 1.8 collective-permute-start.3
  332.6 9.9 %collective-permute-done.3 = f32[1,7,128,128]{3,1,2,0:T(8,128)S(1)} collective-permute-done((f32[1,7,128,128]{3,1,2,0:T(8,128)S(1)}, f32[1,7,128,128]{3,1,2,0:T(8,128)S(1)}, u32[]{:S(2)}, u32[]{:S(2)}) %collective-permute-start.3) | collective-permute-done | bytes 458784 | tf_op jit(solution)/shard_map/ppermute | solution.py:18
  342.6 3.4 fusion.42
  346.0 2.5 copy.59
  348.5 7.2 %all-to-all-start = ((f32[8,7,128,128]{3,2,1,0:T(8,128)}), f32[8,7,128,128]{3,2,1,0:T(8,128)}, u32[]{:S(2)}, u32[]{:S(2)}) async-start(f32[8,7,128,128]{3,2,1,0:T(8,128)} %copy.59), calls=%async_computation | async-start | bytes 7340032 | tf_op jit(solution)/shard_map/all_to_all | solution.py:101
  356.0 0.7 gather_fusion.3
  357.2 0.7 gather_fusion.4
  358.3 1.8 gather_fusion.5
  360.2 38.9 %all-to-all-done = f32[8,7,128,128]{3,2,1,0:T(8,128)} async-done(((f32[8,7,128,128]{3,2,1,0:T(8,128)}), f32[8,7,128,128]{3,2,1,0:T(8,128)}, u32[]{:S(2)}, u32[]{:S(2)}) %all-to-all-start) | async-done | bytes 3670048 | tf_op jit(solution)/shard_map/all_to_all | solution.py:101
  399.0 5.5 %fusion.48 = f32[8,1,128,1]{2,1,3,0:T(1,128)S(1)} fusion(f32[8,7,128,128]{3,2,1,0:T(8,128)} %all-to-all-done, f32[8,7,128,1]{2,1,0,3:T(8,128)S(1)} %select_bitcast_fusion.1), kind=kOutput, calls=%fused_computation.80 | convolution fusion | flops 11010048 | bytes 3702784 | tf_op jit(solution)/shard_map/gsmn,gsn->gm/dot_general | solution.py:124
  404.7 39.3 %all_to_all.27 = f32[256,8,128]{2,1,0:T(8,128)S(1)} all-to-all(f32[256,8,128]{2,1,0:T(8,128)S(1)} %stack.5), channel_id=1, replica_groups=mesh['grp'=8,'row'=32] {'grp','row'}, dimensions={0} | all-to-all | bytes 2097152 | tf_op jit(solution)/shard_map/all_to_all | solution.py:118
  444.6 5.6 %fusion.46 = f32[8,1,128,1]{2,1,3,0:T(1,128)S(1)} fusion(f32[8,7,128,128]{3,2,1,0:T(8,128)} %all-to-all-done, f32[8,7,128,1]{2,1,0,3:T(8,128)S(1)} %select_bitcast_fusion), kind=kOutput, calls=%fused_computation.78 | convolution fusion | flops 11010048 | bytes 3702784 | tf_op jit(solution)/shard_map/gsmn,gsn->gm/dot_general | solution.py:124
  450.8 4.3 copy.118
  (136 shorter events, 10.4 us)
Async XLA Ops:
  0.6 12.2 %copy-start = (f32[4,128]{1,0:T(4,128)S(1)}, f32[4,128]{1,0:T(4,128)}, u32[]{:S(2)}) copy-start(f32[4,128]{1,0:T(4,128)} %param.27) | copy-start | bytes 6148
  2.9 35.8 %collective-permute-start = (bf16[10,2,128,128]{3,2,1,0:T(8,128)(2,1)}, bf16[10,2,128,128]{3,2,1,0:T(8,128)(2,1)}, u32[]{:S(2)}, u32[]{:S(2)}) collective-permute-start(bf16[10,2,128,128]{3,2,1,0:T(8,128)(2,1)} %get-tuple-element.459), channel_id=1, source_target_pairs={{0,1},{1,2},{2,3},{3,4},{4,5},{5,6},{6,7},{7,8},{8,9},{9,10},{10,1... | collective-permute-start | bytes 1966088 | tf_op jit(solution)/shard_map/ppermute | solution.py:15
  4.9 33.7 %collective-permute-start.1 = (bf16[10,2,128,128]{3,2,1,0:T(8,128)(2,1)S(1)}, bf16[10,2,128,128]{3,2,1,0:T(8,128)(2,1)}, u32[]{:S(2)}, u32[]{:S(2)}) collective-permute-start(bf16[10,2,128,128]{3,2,1,0:T(8,128)(2,1)S(1)} %get-tuple-element.460), channel_id=1, source_target_pairs={{1,0},{2,1},{3,2},{4,3},{5,4},{6,5},{7,6},{8,7},{9,8},{10,9},{11,1... | collective-permute-start | bytes 1966088 | tf_op jit(solution)/shard_map/ppermute | solution.py:18
  13.7 14.2 %all-to-all-start.1 = ((f32[8,1,128]{2,1,0:T(1,128)}), f32[8,1,128]{2,1,0:T(1,128)S(1)}, u32[]{:S(2)}, u32[]{:S(2)}) async-start(f32[8,1,128]{2,1,0:T(1,128)} %bitcast.7), calls=%async_computation.1 | async-start | bytes 8192 | tf_op jit(solution)/shard_map/all_to_all | solution.py:102
  19.2 19.5 %copy-start.3 = (bf16[40,2,128,128]{3,2,1,0:T(8,128)(2,1)S(1)}, bf16[40,2,128,128]{3,2,1,0:T(8,128)(2,1)}, u32[]{:S(2)}) copy-start(bf16[40,2,128,128]{3,2,1,0:T(8,128)(2,1)} %param.25) | copy-start | bytes 7864324
  27.8 14.1 %copy-start.7 = (f32[8,1,128]{2,1,0:T(1,128)}, f32[8,1,128]{2,1,0:T(1,128)S(1)}, u32[]{:S(2)}) copy-start(f32[8,1,128]{2,1,0:T(1,128)S(1)} %all-to-all-done.1) | copy-start | bytes 12292
  28.9 319.6 %all-to-all-start.2 = ((f32[256,8,128]{2,1,0:T(8,128)}), f32[256,8,128]{2,1,0:T(8,128)}, u32[]{:S(2)}, u32[]{:S(2)}) async-start(f32[256,8,128]{2,1,0:T(8,128)} %stack.4), calls=%async_computation.2 | async-start | bytes 2097152 | tf_op jit(solution)/shard_map/all_to_all | solution.py:118
  38.6 3.3 copy-start.6
  70.0 10.6 %copy-start.4 = (bf16[40,2,128,128]{3,2,1,0:T(8,128)(2,1)S(1)}, bf16[40,2,128,128]{3,2,1,0:T(8,128)(2,1)}, u32[]{:S(2)}) copy-start(bf16[40,2,128,128]{3,2,1,0:T(8,128)(2,1)} %get-tuple-element.600) | copy-start | bytes 7864324 | tf_op jit(solution)/shard_map/while
  136.3 10.6 %copy-start.4 = (bf16[40,2,128,128]{3,2,1,0:T(8,128)(2,1)S(1)}, bf16[40,2,128,128]{3,2,1,0:T(8,128)(2,1)}, u32[]{:S(2)}) copy-start(bf16[40,2,128,128]{3,2,1,0:T(8,128)(2,1)} %get-tuple-element.600) | copy-start | bytes 7864324 | tf_op jit(solution)/shard_map/while
  202.6 10.6 %copy-start.4 = (bf16[40,2,128,128]{3,2,1,0:T(8,128)(2,1)S(1)}, bf16[40,2,128,128]{3,2,1,0:T(8,128)(2,1)}, u32[]{:S(2)}) copy-start(bf16[40,2,128,128]{3,2,1,0:T(8,128)(2,1)} %get-tuple-element.600) | copy-start | bytes 7864324 | tf_op jit(solution)/shard_map/while
  268.9 10.6 %copy-start.4 = (bf16[40,2,128,128]{3,2,1,0:T(8,128)(2,1)S(1)}, bf16[40,2,128,128]{3,2,1,0:T(8,128)(2,1)}, u32[]{:S(2)}) copy-start(bf16[40,2,128,128]{3,2,1,0:T(8,128)(2,1)} %get-tuple-element.600) | copy-start | bytes 7864324 | tf_op jit(solution)/shard_map/while
  307.4 3.4 copy-start.5
  311.6 19.1 %collective-permute-start.2 = (f32[1,7,128,128]{3,1,2,0:T(8,128)S(1)}, f32[1,7,128,128]{3,1,2,0:T(8,128)S(1)}, u32[]{:S(2)}, u32[]{:S(2)}) collective-permute-start(f32[1,7,128,128]{3,1,2,0:T(8,128)S(1)} %slice.195), channel_id=1, source_target_pairs={{0,1},{1,2},{2,3},{3,4},{4,5},{5,6},{6,7},{7,8},{8,9},{9,10},{10,1... | collective-permute-start | bytes 1376264 | tf_op jit(solution)/shard_map/ppermute | solution.py:15
  330.8 11.7 %collective-permute-start.3 = (f32[1,7,128,128]{3,1,2,0:T(8,128)S(1)}, f32[1,7,128,128]{3,1,2,0:T(8,128)S(1)}, u32[]{:S(2)}, u32[]{:S(2)}) collective-permute-start(f32[1,7,128,128]{3,1,2,0:T(8,128)S(1)} %get-tuple-element.457), channel_id=1, source_target_pairs={{1,0},{2,1},{3,2},{4,3},{5,4},{6,5},{7,6},{8,7},{9,8},{10,9},{11,1... | collective-permute-start | bytes 1376264 | tf_op jit(solution)/shard_map/ppermute | solution.py:18
  348.5 7.5 %copy-start.2 = (s32[1024]{0:T(1024)S(1)}, s32[1024]{0:T(1024)}, u32[]{:S(2)}) copy-start(s32[1024]{0:T(1024)} %param.26) | copy-start | bytes 12292
  348.5 50.5 %all-to-all-start = ((f32[8,7,128,128]{3,2,1,0:T(8,128)}), f32[8,7,128,128]{3,2,1,0:T(8,128)}, u32[]{:S(2)}, u32[]{:S(2)}) async-start(f32[8,7,128,128]{3,2,1,0:T(8,128)} %copy.59), calls=%async_computation | async-start | bytes 7340032 | tf_op jit(solution)/shard_map/all_to_all | solution.py:101
  357.2 47.4 %copy-start.8 = (f32[8,1,128]{2,1,0:T(1,128)S(1)}, f32[8,1,128]{2,1,0:T(1,128)}, u32[]{:S(2)}) copy-start(f32[8,1,128]{2,1,0:T(1,128)} %copy-done.7) | copy-start | bytes 12292
  404.6 45.6 %copy-start.9 = (f32[8,128]{1,0:T(8,128)}, f32[8,128]{1,0:T(8,128)S(1)}, u32[]{:S(2)}) copy-start(f32[8,128]{1,0:T(8,128)S(1)} %fusion.50) | copy-start | bytes 12292
  450.2 4.9 %copy-start.1 = (f32[4,128]{1,0:T(4,128)S(1)}, f32[4,128]{1,0:T(4,128)}, u32[]{:S(2)}) copy-start(f32[4,128]{1,0:T(4,128)} %param.27) | copy-start | bytes 6148
